TPU v7x, 128 devices: a whole 4x4x4 slice. The times are simulated.
128 devices in a mesh: hi: 16 (over y, x), lo: 8 (over z, core).
Axes of the slice: x: 4, y: 4, z: 4, core: 2. Of those that a mesh axis runs over, the one named last changes fastest.
Arguments:
- previous: float32 [32, 2097152], P(None, ('hi', 'lo')), may hold values from -6 to 6
- current: float32 [32, 2097152], P(None, ('hi', 'lo')), may hold values from -6 to 6
- field_levels: int32 [21], replicated, may hold values from -4 to 4
- bond_levels: int32 [20], replicated, may hold values from 1 to 3
Outputs:
- ortho_block: float32 [32, 2097152], P(None, ('hi', 'lo'))
- upper_factor: float32 [32, 32], replicated
All inputs are finite; a program needn't handle non-finite values.
Results may differ from a plain program's by a relative error of at most 0.00005.
Values sent between devices are 32-bit elements; how exact they have to be, the bound alone decides.
A program may use at most 64 MiB of HBM per device.

v0:
```python
import jax
import jax.numpy as jnp
from jax import lax
from jax.sharding import PartitionSpec as P

FIELD_STEP = 0.75
COUPLING_STEP = 0.5


def chain_matrix(couplings, bit_count, bond_list):
    width = 2**bit_count
    rows = lax.iota(jnp.int32, width)[:, None]
    cols = lax.iota(jnp.int32, width)[None, :]
    matrix = jnp.zeros((width, width), jnp.float32)
    for site_number, spot in bond_list:
        differ = cols >> spot & 1 != cols >> spot + 1 & 1
        target = rows == cols ^ 3 << spot
        matrix = matrix + jnp.where(differ & target, 0.5 * couplings[site_number], 0.0)
    return matrix


def cross_flip(values, coupling, low_spot):
    width = values.shape[-1]
    index = lax.iota(jnp.int32, width)
    permute = (index[:, None] == index[None, :] ^ 1 << low_spot).astype(jnp.float32)
    moved = jnp.einsum("vatbl,lj->vatbj", values, permute, precision=lax.Precision.HIGHEST)
    flipped = jnp.flip(moved, axis=2)
    upper = lax.iota(jnp.int32, 2)[:, None]
    keep = (index[None, :] >> low_spot & 1 != upper).astype(jnp.float32)
    return 0.5 * coupling * flipped * keep[None, None, :, None, :]


def local(previous, current, field_levels, bond_levels):
    vectors, amp_count = current.shape
    site_count = field_levels.shape[0]
    devices = lax.axis_size("hi") * lax.axis_size("lo")
    local_bits = amp_count.bit_length() - 1
    global_bits = devices.bit_length() - 1
    rest_bits = local_bits - global_bits
    device = lax.axis_index("hi") * lax.axis_size("lo") + lax.axis_index("lo")
    local_index = lax.iota(jnp.int32, amp_count)
    top_width = 2**global_bits
    low_width = 2**rest_bits

    def position(site_number):
        if site_number < global_bits:
            return rest_bits + site_number
        return site_number - global_bits

    def spin_value(site_number):
        if site_number < local_bits:
            return 0.5 - (local_index >> position(site_number) & 1).astype(jnp.float32)
        return 0.5 - (device >> site_number - local_bits & 1).astype(jnp.float32)

    fields = FIELD_STEP * field_levels.astype(jnp.float32)
    couplings = COUPLING_STEP * bond_levels.astype(jnp.float32)
    diagonal = jnp.zeros((amp_count,), jnp.float32)
    for site_number in range(site_count):
        diagonal = diagonal + fields[site_number] * spin_value(site_number)
        if site_number < site_count - 1:
            diagonal = diagonal + couplings[site_number] * spin_value(site_number) * spin_value(
                site_number + 1
            )
    top_matrix = chain_matrix(
        couplings,
        global_bits,
        [(site_number, site_number) for site_number in range(global_bits - 1)],
    )
    low_matrix = chain_matrix(
        couplings,
        rest_bits,
        [
            (site_number, site_number - global_bits)
            for site_number in range(global_bits, local_bits - 1)
        ],
    )
    blocks = current.reshape(vectors, top_width, low_width)
    applied = diagonal[None, :] * current
    applied = applied + jnp.einsum(
        "vtl,tu->vul", blocks, top_matrix, precision=lax.Precision.HIGHEST
    ).reshape(vectors, amp_count)
    applied = applied + jnp.einsum(
        "vtl,lu->vtu", blocks, low_matrix, precision=lax.Precision.HIGHEST
    ).reshape(vectors, amp_count)
    joined = cross_flip(
        current.reshape(vectors, 1, 2, top_width // 2, low_width), couplings[global_bits - 1], 0
    )
    applied = applied + joined.reshape(vectors, amp_count)
    far_matrix = chain_matrix(
        couplings,
        global_bits,
        [
            (site_number, site_number - local_bits)
            for site_number in range(local_bits, site_count - 1)
        ],
    )
    shaped = current.reshape(vectors, devices, amp_count // devices)
    arrived = lax.all_to_all(shaped, ("hi", "lo"), split_axis=1, concat_axis=1, tiled=True)
    count = arrived.shape[0]
    bond_terms = jnp.einsum(
        "vtl,tu->vul", arrived, far_matrix, precision=lax.Precision.HIGHEST
    ).reshape(count, amp_count)
    seam = cross_flip(
        arrived.reshape(count, top_width // 2, 2, 1, low_width),
        couplings[local_bits - 1],
        rest_bits - 1,
    )
    bond_terms = bond_terms + seam.reshape(count, amp_count)
    remote_part = lax.all_to_all(
        bond_terms.reshape(arrived.shape), ("hi", "lo"), split_axis=1, concat_axis=1, tiled=True
    ).reshape(vectors, amp_count)
    filtered = 4.0 / site_count * (applied + remote_part) - previous
    local_gram = jnp.dot(filtered, filtered.T, precision=lax.Precision.HIGHEST) / (
        amp_count * devices
    )
    gram_matrix = lax.psum(local_gram, ("hi", "lo"))
    lower_factor = jnp.linalg.cholesky(gram_matrix)
    inverse = jax.scipy.linalg.solve_triangular(
        lower_factor, jnp.eye(vectors, dtype=jnp.float32), lower=True
    )
    ortho_block = jnp.dot(inverse, filtered, precision=lax.Precision.HIGHEST)
    return (ortho_block, lower_factor.T)


def solution(mesh):
    in_specs = (P(None, ("hi", "lo")), P(None, ("hi", "lo")), P(), P())
    out_specs = (P(None, ("hi", "lo")), P())
    return jax.shard_map(local, mesh=mesh, in_specs=in_specs, out_specs=out_specs, check_vma=False)
```

profile of v0, /device:TPU:1, one launch (start us, length us, event | category | flops | bytes accessed | tf_op | source)
XLA Modules:
  0.0 200.1 jit_solution(15617030087911046846)
XLA Ops:
  0.6 3.2 %copy_bitcast_fusion = f32[32,128,128]{2,0,1:T(8,128)} fusion(f32[32,16384]{1,0:T(8,128)} %param.5), kind=kLoop, calls=%fused_computation.6 | loop fusion | bytes 4194304 | tf_op jit(solution)/shard_map/reshape | solution.py:77
  3.8 0.0 copy-start
  3.8 0.0 copy-start.1
  3.8 11.5 %all-to-all-start = ((f32[32,128,128]{2,0,1:T(8,128)}), f32[32,128,128]{2,0,1:T(8,128)S(1)}, u32[]{:S(2)}, u32[]{:S(2)}) async-start(f32[32,128,128]{2,0,1:T(8,128)} %copy_bitcast_fusion), calls=%async_computation | async-start | bytes 4194304 | tf_op jit(solution)/shard_map/all_to_all | solution.py:98
  15.3 0.0 copy-done
  15.4 0.7 fusion.153
  20.4 0.0 copy-done.1
  20.4 25.0 %all-to-all-done = f32[32,128,128]{2,0,1:T(8,128)S(1)} async-done(((f32[32,128,128]{2,0,1:T(8,128)}), f32[32,128,128]{2,0,1:T(8,128)S(1)}, u32[]{:S(2)}, u32[]{:S(2)}) %all-to-all-start) | async-done | bytes 2097184 | tf_op jit(solution)/shard_map/all_to_all | solution.py:98
  45.4 2.3 %fusion.7 = f32[32,64,2,128]{3,1,2,0:T(8,128)S(1)} fusion(f32[32,64,2,128]{3,0,2,1:T(8,128)S(1)} %bitcast.129, s32[128]{0:T(128)S(1)} %iota_xor_fusion), kind=kOutput, calls=%fused_computation.14 | convolution fusion | flops 805322752 | bytes 4194816 | tf_op jit(solution)/shard_map/vatbl,lj->vatbj/dot_general | solution.py:26
  47.7 0.3 multiply_multiply_fusion
  48.1 1.7 copy.31
  49.8 3.2 %bitcast_add_fusion.3 = f32[32,128,128]{2,1,0:T(8,128)S(1)} fusion(f32[32,128,128]{2,1,0:T(8,128)S(1)} %bitcast.133, f32[32,128,128]{2,0,1:T(8,128)S(1)} %all-to-all-done, f32[]{:T(128)S(6)} %mul.670, f32[]{:T(128)S(6)} %mul.669, f32[]{:T(128)S(6)} %mul.668, f32[]{:T(128)S(6)} %mul.667, f32[]{:T(128)S(6)} %mul.666, f32[]{:T(128)S(6)} %mul.665, ...), kind=kOutput, calls=%fused_computation.7 | convolution fusion | flops 806207488 | bytes 6295320 | tf_op jit(solution)/shard_map/vtl,tu->vul/dot_general | solution.py:100
  53.0 2.5 %copy.32 = f32[32,128,128]{2,0,1:T(8,128)} copy(f32[32,128,128]{2,1,0:T(8,128)S(1)} %bitcast_add_fusion.3) | data formatting | bytes 4194304 | tf_op jit(solution)/shard_map/add | solution.py:108
  55.5 5.9 %all-to-all-start.1 = ((f32[32,128,128]{2,0,1:T(8,128)}), f32[32,128,128]{2,0,1:T(8,128)}, u32[]{:S(2)}, u32[]{:S(2)}) async-start(f32[32,128,128]{2,0,1:T(8,128)} %copy.32), calls=%async_computation.1 | async-start | bytes 4194304 | tf_op jit(solution)/shard_map/all_to_all | solution.py:109
  61.4 0.7 fusion.151
  74.1 2.0 copy.42
  76.1 3.4 %convolution_bitcast_fusion.1 = f32[32,128,128]{1,2,0:T(8,128)} fusion(f32[32,128,128]{2,1,0:T(8,128)S(1)} %bitcast.125, f32[]{:T(128)S(6)} %mul.659, f32[]{:T(128)S(6)} %mul.658, f32[]{:T(128)S(6)} %mul.657, f32[]{:T(128)S(6)} %mul.656, f32[]{:T(128)S(6)} %mul.655, f32[]{:T(128)S(6)} %mul.654, s32[128]{0:T(128)S(1)} %get-tuple-element.52, ...), kind=kOutput, calls=%fused_computation.16 | convolution fusion | flops 805683200 | bytes 4198168 | tf_op jit(solution)/shard_map/vtl,lu->vtu/dot_general | solution.py:82
  79.5 2.9 %copy.27 = f32[32,128,128]{2,1,0:T(8,128)} copy(f32[32,128,128]{1,2,0:T(8,128)} %convolution_bitcast_fusion.1) | data formatting | bytes 4194304 | tf_op jit(solution)/shard_map/vtl,lu->vtu/dot_general | solution.py:82
  86.2 0.6 fusion.152
  86.7 17.3 %add_add_fusion = f32[16384]{0:T(1024)S(1)} fusion(f32[]{:T(128)S(6)} %mul.645, f32[]{:T(128)S(6)} %mul.644, f32[]{:T(128)S(6)} %mul.642, f32[]{:T(128)S(6)} %mul.641, f32[]{:T(128)S(6)} %mul.639, f32[]{:T(128)S(6)} %mul.638, f32[]{:T(128)S(6)} %mul.636, f32[]{:T(128)S(6)} %mul.635, f32[]{:T(128)S(6)} %mul.633, f32[]{:T(128)S(6)} %mul.632, f32[]{:T(128)S(6)} %mul.630, ...), kind=kLoop, calls=%fused_computation.63 | loop fusion | flops 2260992 | bytes 65704 | tf_op jit(solution)/shard_map/add | solution.py:59
  104.1 1.1 convolution_bitcast_fusion
  105.2 1.6 multiply_multiply_fusion.1
  106.8 3.4 %fusion.14 = f32[128,32,128]{2,0,1:T(8,128)} fusion(f32[32,128,128]{2,1,0:T(8,128)S(1)} %bitcast.127, f32[]{:T(128)S(6)} %mul.653, s32[128]{0:T(128)S(1)} %get-tuple-element.52, f32[]{:T(128)S(6)} %mul.652, s32[128]{0:T(128)S(1)} %get-tuple-element.53, f32[]{:T(128)S(6)} %mul.651, s32[128]{0:T(128)S(1)} %get-tuple-element.54, f32[]{:T(128)S(6)} %mul.650, ...), kind=kOutput, calls=%fused_computation.20 | convolution fusion | flops 805683200 | bytes 4198168 | tf_op jit(solution)/shard_map/vtl,tu->vul/dot_general | solution.py:79
  110.2 0.0 all-to-all-done.1
  110.2 9.6 %fusion.2 = f32[32,16384]{1,0:T(8,128)S(1)} fusion(f32[32,16384]{1,0:T(8,128)} %param.4, f32[4,8,128,128]{3,2,1,0:T(8,128)} %bitcast.130, f32[4,8,128,128]{3,2,1,0:T(8,128)} %bitcast.132, f32[4,8,128,128]{3,2,1,0:T(8,128)} %bitcast.131, f32[32,16384]{1,0:T(8,128)} %param.5, f32[16384]{0:T(1024)S(1)} %add_add_fusion, f32[32,128,128]{2,0,1:T(8,128)} %all-to-all-done.1), kind=kLoop, calls=%fused_computation.3 | loop fusion | flops 3670016 | bytes 14745600 | tf_op jit(solution)/shard_map/sub | solution.py:112
  119.8 1.8 convolution_multiply_fusion
  121.6 67.6 %psum.7 = f32[32,32]{0,1:T(8,128)S(1)} all-reduce(f32[32,32]{0,1:T(8,128)S(1)} %convolution_multiply_fusion), channel_id=1, replica_groups=mesh['hi'=16,'lo'=8] {'hi','lo'}, use_global_device_ids=true, to_apply=%region_0.1 | all-reduce | flops 1024 | bytes 8192 | tf_op jit(solution)/shard_map/psum | solution.py:116
  189.2 0.1 copy.35
  189.3 2.9 %cholesky.17 = f32[32,32]{1,0:T(8,128)S(1)} custom-call(f32[32,32]{1,0:T(8,128)S(1)} %fusion.138), custom_call_target="Cholesky" | custom-call | tf_op jit(solution)/shard_map/jit(cholesky)/cholesky | solution.py:117
  192.2 0.6 compare_reduce_fusion
  192.9 0.7 fusion.139
  193.5 2.4 %custom-call.7 = f32[1,32,32]{1,2,0:T(8,128)S(1)} custom-call(f32[1,32,32]{2,1,0:T(8,128)S(1)} %get-tuple-element.11), custom_call_target="InvertDiagBlocksLowerTriangular" | custom-call | tf_op jit(solution)/shard_map/jit(_solve_triangular)/triangular_solve | solution.py:118
  196.0 0.2 fusion.136
  196.2 3.2 %fusion.154 = f32[32,16384]{1,0:T(8,128)} fusion(f32[32,32]{1,0:T(8,128)S(1)} %fusion.136, f32[32,16384]{1,0:T(8,128)S(1)} %fusion.2), kind=kOutput, calls=%fused_computation.175 | convolution fusion | flops 201326592 | bytes 4198400 | tf_op jit(solution)/shard_map/dot_general | solution.py:121
  199.4 0.7 copy.36
  (16 shorter events, 0.1 us)
Async XLA Ops:
  3.8 11.5 %copy-start = (s32[20]{0:T(128)S(1)}, s32[20]{0:T(128)}, u32[]{:S(2)}) copy-start(s32[20]{0:T(128)} %param.7) | copy-start | bytes 244
  3.8 16.6 %copy-start.1 = (s32[21]{0:T(128)S(1)}, s32[21]{0:T(128)}, u32[]{:S(2)}) copy-start(s32[21]{0:T(128)} %param.6) | copy-start | bytes 256
  3.8 41.6 %all-to-all-start = ((f32[32,128,128]{2,0,1:T(8,128)}), f32[32,128,128]{2,0,1:T(8,128)S(1)}, u32[]{:S(2)}, u32[]{:S(2)}) async-start(f32[32,128,128]{2,0,1:T(8,128)} %copy_bitcast_fusion), calls=%async_computation | async-start | bytes 4194304 | tf_op jit(solution)/shard_map/all_to_all | solution.py:98
  55.5 54.7 %all-to-all-start.1 = ((f32[32,128,128]{2,0,1:T(8,128)}), f32[32,128,128]{2,0,1:T(8,128)}, u32[]{:S(2)}, u32[]{:S(2)}) async-start(f32[32,128,128]{2,0,1:T(8,128)} %copy.32), calls=%async_computation.1 | async-start | bytes 4194304 | tf_op jit(solution)/shard_map/all_to_all | solution.py:109
where the time goes:
time: 201 us; the launch traced here: 200 us
  blocking collectives  67.6 us (34%)
  other arithmetic  35.6 us (18%)
  waiting for transfers between devices  25 us (12%)
  between operations  20.7 us (10%)
  matrix products  18.7 us (9%)
  starting transfers between devices  17.4 us (9%)
  local copies, waits for them, and re-layouts  15.1 us (8%)
    psum x1, blocking collectives, local(): gram_matrix = lax.psum(local_gram, ('hi', 'lo'))  67.6 us
    all_to_all x1, waiting for transfers between devices, local(): lax.all_to_all(shaped, ('hi', 'lo'), split_axis=1, concat_axis=1, tiled=T...  25 us
    add x1, other arithmetic, local(): diagonal = diagonal + fields[site_number] * spin_value(site_number)  17.3 us
    all_to_all x1, starting transfers between devices, local(): lax.all_to_all(shaped, ('hi', 'lo'), split_axis=1, concat_axis=1, tiled=T...  11.5 us
    sub x1, other arithmetic, local(): filtered = 4.0 / site_count * (applied + remote_part) - previous  9.63 us
    all_to_all x1, starting transfers between devices, local(): lax.all_to_all(bond_terms.reshape(arrived.shape), ('hi', 'lo'), split_axi...  5.89 us
  transfers between devices with their start and end apart: 2, of which 1 were waited for; matrix products, arithmetic and copies ran while one was open for 17% of the time, Pallas kernels for 0%

commit v1 on v0

v1 whole, which is shorter than its diff:
```python
import functools

import jax
import jax.numpy as jnp
from jax import lax
from jax.experimental import pallas as pl
from jax.experimental.pallas import tpu as pltpu
from jax.sharding import PartitionSpec as P

MESH = pl.DeviceIdType.MESH
HIGHEST = lax.Precision.HIGHEST
VECTORS = 32
AMPS = 16384
TOTAL = 2097152
SITES = 21
SCALE = 4.0 / SITES
CHUNKS = 16
WIDTH = AMPS // CHUNKS
TOPS = WIDTH // 128
LEAD = 2
LAST_LAG = 3


def far_kernel(
    field_ref, bond_ref, previous_hbm, current_hbm, filtered_hbm, gram_ref,
    current, previous, filtered, weights, direct, ring_z, ring_x, gram, first, second,
    load_sem, send_sem, relay_sem, direct_sem, z_sem, x_sem, small_send, first_sem, second_sem,
):
    hi = lax.axis_index("hi")
    lo = lax.axis_index("lo")
    core = lo & 1
    z = lo >> 1
    x = hi & 3
    y = hi >> 2
    z0, z1, x0, x1, y0, y1 = z & 1, z >> 1, x & 1, x >> 1, y & 1, y >> 1

    load_current = pltpu.make_async_copy(current_hbm, current, load_sem.at[0])
    load_previous = pltpu.make_async_copy(previous_hbm, previous, load_sem.at[1])
    load_current.start()
    load_previous.start()

    barrier = pltpu.get_barrier_semaphore()
    for i in range(1, 8):
        pl.semaphore_signal(barrier, inc=1, device_id=(hi, lo ^ i), device_id_type=MESH)
    for i in range(1, 16):
        pl.semaphore_signal(barrier, inc=1, device_id=(hi ^ i, lo), device_id_type=MESH)
    pl.semaphore_wait(barrier, 22)

    def columns(k):
        return pl.ds(pl.multiple_of(k * WIDTH, WIDTH), WIDTH)

    partners = [(hi, lo ^ 1), (hi, lo ^ 3), (hi, lo ^ 6), (hi ^ 3, lo), (hi ^ 12, lo)]
    takes = [None, core != z0, z0 != z1, x0 != x1, y0 != y1]

    def when(condition, body):
        if condition is None:
            body()
        else:
            pl.when(condition)(body)

    def direct_copy(i, cols, sem):
        return pltpu.make_async_remote_copy(
            src_ref=current_hbm.at[:, cols], dst_ref=direct.at[i, :, cols],
            send_sem=send_sem.at[i], recv_sem=sem, device_id=partners[i], device_id_type=MESH,
        )

    first_path = core == 0

    def ring_plan(spot, pair_bit, ring_device, pair_device):
        role = jnp.where(pair_bit == 1, spot, 3 - spot)

        def at_role(r):
            return ring_device(jnp.where(pair_bit == 1, r, 3 - r))

        def pick(condition, a, b):
            return tuple(jnp.where(condition, u, v) for u, v in zip(a, b))

        own_device = pick(first_path, at_role(jnp.where(role == 0, 3, 0)), pair_device)
        last_a = jnp.where(first_path, 2, 0)
        last_b = jnp.where(first_path, 0, 2)
        has_a = (role == 3) | (role == last_a)
        has_b = (role == 3) | (role == last_b)
        a_device = pick(
            first_path,
            pick(role == 3, at_role(2), pair_device),
            pick(role == 3, at_role(0), at_role(1)),
        )
        b_device = pick(
            first_path,
            pick(role == 3, pair_device, at_role(3)),
            pick(role == 3, at_role(0), at_role(3)),
        )
        return dict(
            active=role < 2, own=(own_device, jnp.where(role == 0, 0, 1)),
            relays=[
                (has_a, a_device, jnp.where(role == 3, 0, 2), jnp.where(role == 3, 1, 2)),
                (has_b, b_device, jnp.where(role == 3, 2, 1), jnp.where(role == 3, 2, 1)),
            ],
        )

    plans = [
        (ring_z, z_sem, 5, 0, ring_plan(z, x0, lambda s: (hi, s * 2 + core), (hi ^ 1, lo))),
        (ring_x, x_sem, 6, 2, ring_plan(x, y0, lambda s: (y * 4 + s, lo), (hi ^ 4, lo))),
    ]

    def own_copy(ring, k_cols, sem_index, plan, recv):
        device, slot = plan["own"]
        return pltpu.make_async_remote_copy(
            src_ref=current_hbm.at[:, k_cols], dst_ref=ring.at[slot, :, k_cols],
            send_sem=send_sem.at[sem_index], recv_sem=recv, device_id=device, device_id_type=MESH,
        )

    def relay_copy(ring, which, k_cols, sem_index, relay, recv):
        _, device, slot, _ = relay
        return pltpu.make_async_remote_copy(
            src_ref=ring.at[which, :, k_cols], dst_ref=ring.at[slot, :, k_cols],
            send_sem=relay_sem.at[sem_index], recv_sem=recv, device_id=device, device_id_type=MESH,
        )

    def arrived(ring, slot, sems, k):
        cols = columns(k)
        pltpu.make_async_remote_copy(
            src_ref=ring.at[slot, :, cols], dst_ref=ring.at[slot, :, cols],
            send_sem=relay_sem.at[0], recv_sem=sems.at[slot, k],
            device_id=(hi, lo ^ 1), device_id_type=MESH,
        ).wait_recv()

    def send_own(k):
        cols = columns(k)
        for ring, sems, index, _, plan in plans:
            slot = plan["own"][1]
            when(plan["active"], lambda ring=ring, sems=sems, index=index, plan=plan, slot=slot:
                 own_copy(ring, cols, index, plan, sems.at[slot, k]).start())
        when(takes[1], lambda: direct_copy(1, cols, direct_sem.at[1, k]).start())

    @pl.loop(0, LEAD)
    def _(k):
        send_own(k)

    @pl.loop(0, CHUNKS)
    def _(k):
        cols = columns(k)
        for i in (2, 3, 4, 0):
            when(takes[i], lambda i=i: direct_copy(i, cols, direct_sem.at[i, k]).start())

    level = [bond_ref[s].astype(jnp.float32) for s in range(SITES - 1)]
    field = [0.75 * field_ref[s].astype(jnp.float32) for s in range(SITES)]
    half = [0.25 * v for v in level]
    full = [0.5 * v for v in level]

    def spin(bit):
        return 0.5 - bit.astype(jnp.float32)

    rows = lax.broadcasted_iota(jnp.int32, (128, 128), 0)
    lanes = lax.broadcasted_iota(jnp.int32, (128, 128), 1)
    flips = jnp.zeros((128, 128), jnp.float32)
    for s in range(7, 13):
        b = s - 7
        hit = (((lanes >> b) ^ (lanes >> (b + 1))) & 1 == 1) & (rows == lanes ^ (3 << b))
        flips = flips + jnp.where(hit, half[s], 0.0)
    lane_diagonal = jnp.zeros((128, 128), jnp.float32)
    for s in range(7, 14):
        lane_diagonal = lane_diagonal + field[s] * spin(lanes >> (s - 7) & 1)
        if s < 13:
            lane_diagonal = lane_diagonal + full[s] * spin(lanes >> (s - 7) & 1) * spin(
                lanes >> (s - 6) & 1
            )
    lane_diagonal = lane_diagonal + full[13] * spin(core) * spin(lanes >> 6 & 1)
    for top in range(2):
        seam = lane_diagonal + full[6] * (0.5 - top) * spin(lanes & 1)
        weights[top, 0:128, :] = flips + jnp.where(rows == lanes, seam, 0.0)
        hit = (rows == lanes ^ 1) & (lanes & 1 != top)
        weights[top, 128:256, :] = jnp.where(hit, half[6], 0.0)
    bits = [core, z0, z1, x0, x1, y0, y1]
    device_part = field[20] * spin(y1)
    for i in range(6):
        device_part = device_part + field[14 + i] * spin(bits[i])
        device_part = device_part + full[14 + i] * spin(bits[i]) * spin(bits[i + 1])

    lane = lax.broadcasted_iota(jnp.int32, (VECTORS, WIDTH), 1)
    core_factor = jnp.where((lane >> 6 & 1) != core, SCALE * half[13], 0.0)
    gram[...] = jnp.zeros_like(gram)

    def top_columns(t):
        return pl.ds(pl.multiple_of(t * 128, 128), 128)

    def local_part(k):
        sums = []
        left = []
        for i in range(TOPS):
            t = k * TOPS + i
            spins = [spin(t >> s & 1) for s in range(7)]
            diagonal = device_part + field[6] * spins[6]
            for s in range(6):
                diagonal = diagonal + field[s] * spins[s] + full[s] * spins[s] * spins[s + 1]
            own = current[:, top_columns(t)]
            total = diagonal * own
            for s in range(6):
                differ = ((t >> s) ^ (t >> (s + 1)) & 1) & 1
                factor = half[s] * differ.astype(jnp.float32)
                total = total + factor * current[:, top_columns(t ^ (3 << s))]
            sums.append(total)
            left.append(jnp.concatenate([own, current[:, top_columns(t ^ 64)]], axis=1))
        product = jnp.dot(
            jnp.concatenate(left, axis=0), weights[k // (CHUNKS // 2)],
            precision=HIGHEST, preferred_element_type=jnp.float32,
        )
        for i in range(TOPS):
            where = top_columns(k * TOPS + i)
            filtered[:, where] = (
                SCALE * (sums[i] + product[i * VECTORS:(i + 1) * VECTORS]) - previous[:, where]
            )

    def consume(k):
        cols = columns(k)

        direct_copy(0, cols, direct_sem.at[0, k]).wait_recv()
        filtered[:, cols] += core_factor * jnp.concatenate(
            [
                pltpu.roll(direct[0, :, top_columns(k * TOPS + i)], 64, 1)
                for i in range(TOPS)
            ],
            axis=1,
        )
        for i, bond in ((1, 14), (2, 15), (3, 17), (4, 19)):
            def add(i=i, bond=bond):
                direct_copy(i, cols, direct_sem.at[i, k]).wait_recv()
                filtered[:, cols] += SCALE * half[bond] * direct[i, :, cols]
            when(takes[i], add)
        for (ring, sems, _, _, plan), bond in zip(plans, (16, 18)):
            def add(ring=ring, sems=sems, bond=bond):
                arrived(ring, 2, sems, k)
                filtered[:, cols] += SCALE * half[bond] * ring[2, :, cols]
            when(plan["active"], add)
        part = filtered[:, cols]
        gram[...] += lax.dot_general(
            part, part, (((1,), (1,)), ((), ())), precision=HIGHEST,
            preferred_element_type=jnp.float32,
        )

    load_current.wait()
    load_previous.wait()

    @pl.loop(0, CHUNKS + LAST_LAG)
    def _(s):
        @pl.when(s + LEAD < CHUNKS)
        def _():
            send_own(s + LEAD)

        for ring, sems, _, base, plan in plans:
            for which in range(2):
                relay = plan["relays"][which]
                has, _, slot, lag = relay
                k = s - lag

                @pl.when(has & (k >= 0) & (k < CHUNKS))
                def _(ring=ring, sems=sems, base=base, which=which, relay=relay, slot=slot, k=k):
                    arrived(ring, which, sems, k)
                    relay_copy(
                        ring, which, columns(k), base + which, relay, sems.at[slot, k]
                    ).start()

        @pl.when(s < CHUNKS)
        def _():
            local_part(s)

        @pl.when(s >= LAST_LAG)
        def _():
            consume(s - LAST_LAG)

    store = pltpu.make_async_copy(filtered, filtered_hbm, load_sem.at[0])
    store.start()

    g = gram[...]
    packed = jnp.concatenate([g[8 * i:8 * i + 8, :] for i in range(4)], axis=1)
    for size, spot, box, sems, base, device in (
        (8, lo, first, first_sem, 0, lambda i: (hi, lo ^ i)),
        (16, hi, second, second_sem, 8, lambda i: (hi ^ i, lo)),
    ):
        box[spot] = packed

        def small(i):
            return pltpu.make_async_remote_copy(
                src_ref=box.at[spot], dst_ref=box.at[spot], send_sem=small_send.at[base + i],
                recv_sem=sems.at[spot], device_id=device(i), device_id_type=MESH,
            )

        for i in range(1, size):
            small(i).start()
        for i in range(1, size):
            other = spot ^ i
            pltpu.make_async_remote_copy(
                src_ref=box.at[other], dst_ref=box.at[other], send_sem=small_send.at[base + i],
                recv_sem=sems.at[other], device_id=device(i), device_id_type=MESH,
            ).wait_recv()
        packed = box[0]
        for i in range(1, size):
            packed = packed + box[i]
    gram_ref[...] = packed * (1.0 / TOTAL)

    whole = pl.ds(0, AMPS)
    for i in range(5):
        when(takes[i], lambda i=i: direct_copy(i, whole, direct_sem.at[i, 0]).wait_send())
    for ring, sems, index, base, plan in plans:
        when(plan["active"], lambda ring=ring, sems=sems, index=index, plan=plan:
             own_copy(ring, whole, index, plan, sems.at[0, 0]).wait_send())
        for which in range(2):
            relay = plan["relays"][which]
            when(relay[0], lambda ring=ring, sems=sems, base=base, which=which, relay=relay:
                 relay_copy(ring, which, whole, base + which, relay, sems.at[0, 0]).wait_send())
    for size, spot, box, sems, base, device in (
        (8, lo, first, first_sem, 0, lambda i: (hi, lo ^ i)),
        (16, hi, second, second_sem, 8, lambda i: (hi ^ i, lo)),
    ):
        for i in range(1, size):
            pltpu.make_async_remote_copy(
                src_ref=box.at[spot], dst_ref=box.at[spot], send_sem=small_send.at[base + i],
                recv_sem=sems.at[spot], device_id=device(i), device_id_type=MESH,
            ).wait_send()
    store.wait()


def last_kernel(gram_ref, filtered_ref, ortho_ref, upper_ref, inverse_ref):
    @pl.when(pl.program_id(0) == 0)
    def _():
        packed = gram_ref[...]
        parts = [packed] + [pltpu.roll(packed, 128 - 32 * i, 1) for i in range(1, 4)]
        table = jnp.concatenate(parts, axis=0)
        row = lax.broadcasted_iota(jnp.int32, (VECTORS, 128), 0)
        lane = lax.broadcasted_iota(jnp.int32, (VECTORS, 128), 1)
        table = jnp.where(lane < 32, table, jnp.where(lane - 32 == row, 1.0, 0.0))
        for j in range(VECTORS - 1):
            factor = table[:, j:j + 1] / table[j:j + 1, j:j + 1]
            factor = jnp.where(row[:, 0:1] > j, factor, 0.0)
            table = table - factor * table[j:j + 1, :]
        pivots = jnp.sum(jnp.where(row == lane, table, 0.0), axis=1, keepdims=True)
        table = table / jnp.sqrt(pivots)
        upper_ref[...] = jnp.where(lane >= row, table, 0.0)[:, 0:32]
        inverse_ref[...] = pltpu.roll(table, 96, 1)[:, 0:32]

    ortho_ref[...] = jnp.dot(
        inverse_ref[...], filtered_ref[...], precision=HIGHEST, preferred_element_type=jnp.float32
    )


def local(previous, current, field_levels, bond_levels):
    any_space = pl.BlockSpec(memory_space=pl.ANY)
    block = (VECTORS, AMPS)
    f32 = jnp.float32
    filtered, gram = pl.pallas_call(
        far_kernel,
        out_shape=(jax.ShapeDtypeStruct(block, f32), jax.ShapeDtypeStruct((8, 128), f32)),
        in_specs=[
            pl.BlockSpec(memory_space=pltpu.SMEM), pl.BlockSpec(memory_space=pltpu.SMEM),
            any_space, any_space,
        ],
        out_specs=(any_space, pl.BlockSpec(memory_space=pltpu.VMEM)),
        scratch_shapes=[
            pltpu.VMEM(block, f32), pltpu.VMEM(block, f32), pltpu.VMEM(block, f32),
            pltpu.VMEM((2, 256, 128), f32),
            pltpu.VMEM((5,) + block, f32), pltpu.VMEM((3,) + block, f32),
            pltpu.VMEM((3,) + block, f32),
            pltpu.VMEM((VECTORS, VECTORS), f32),
            pltpu.VMEM((8, 8, 128), f32), pltpu.VMEM((16, 8, 128), f32),
            pltpu.SemaphoreType.DMA((2,)), pltpu.SemaphoreType.DMA((7,)),
            pltpu.SemaphoreType.DMA((4,)), pltpu.SemaphoreType.DMA((5, CHUNKS)),
            pltpu.SemaphoreType.DMA((3, CHUNKS)), pltpu.SemaphoreType.DMA((3, CHUNKS)),
            pltpu.SemaphoreType.DMA((24,)), pltpu.SemaphoreType.DMA((8,)),
            pltpu.SemaphoreType.DMA((16,)),
        ],
        compiler_params=pltpu.CompilerParams(
            collective_id=1, has_side_effects=True, vmem_limit_bytes=44 << 20
        ),
        name="far_and_gram",
    )(field_levels, bond_levels, previous, current)
    tile = 2048
    return tuple(
        pl.pallas_call(
            last_kernel,
            grid=(AMPS // tile,),
            out_shape=(jax.ShapeDtypeStruct(block, f32), jax.ShapeDtypeStruct((32, 32), f32)),
            in_specs=[
                pl.BlockSpec((8, 128), lambda i: (0, 0)),
                pl.BlockSpec((VECTORS, tile), lambda i: (0, i)),
            ],
            out_specs=(
                pl.BlockSpec((VECTORS, tile), lambda i: (0, i)),
                pl.BlockSpec((32, 32), lambda i: (0, 0)),
            ),
            scratch_shapes=[pltpu.VMEM((32, 32), f32)],
            name="factor_and_apply",
        )(gram, filtered)
    )


def solution(mesh):
    in_specs = (P(None, ("hi", "lo")), P(None, ("hi", "lo")), P(), P())
    out_specs = (P(None, ("hi", "lo")), P())
    return jax.shard_map(local, mesh=mesh, in_specs=in_specs, out_specs=out_specs, check_vma=False)
```

time: 201 us -> 107 us (0.53)
  Pallas kernels: 0 us -> 99.8 us
  blocking collectives: 67.6 us -> 0 us
  other arithmetic: 35.6 us -> 0 us
  waiting for transfers between devices: 25 us -> 0 us
  between operations: 20.7 us -> 0.66 us
  matrix products: 18.7 us -> 0 us
  starting transfers between devices: 17.4 us -> 0 us
  local copies, waits for them, and re-layouts: 15.1 us -> 6.41 us
    pallas_call x0 -> x2, Pallas kernels: none -> 99.8 us  [the longest x1 90.2 us: local(): pl.pallas_call(far_kernel, out_shape=(jax.ShapeDtypeStruct(block, f32), j...]
    psum x1 -> x0, blocking collectives: 67.6 us -> none  [local(): gram_matrix = lax.psum(local_gram, ('hi', 'lo'))]
    all_to_all x2 -> x0, waiting for transfers between devices: 25 us -> none  [the longest x1 25 us: local(): lax.all_to_all(shaped, ('hi', 'lo'), split_axis=1, concat_axis=1, tiled=T...]
    dot_general x7 -> x0, matrix products: 18.4 us -> none  [the longest x2 3.43 us: cross_flip(): jnp.einsum('vatbl,lj->vatbj', values, permute, precision=lax.Precision.HI...]
    all_to_all x2 -> x0, starting transfers between devices: 17.4 us -> none  [the longest x1 11.5 us: local(): lax.all_to_all(shaped, ('hi', 'lo'), split_axis=1, concat_axis=1, tiled=T...]
    add x1 -> x0, other arithmetic: 17.3 us -> none  [local(): diagonal = diagonal + fields[site_number] * spin_value(site_number)]
    sub x1 -> x0, other arithmetic: 9.63 us -> none  [local(): filtered = 4.0 / site_count * (applied + remote_part) - previous]
    another operation x4 -> x0, other arithmetic: 6.03 us -> none  [the longest x3 3.59 us: local(): lower_factor = jnp.linalg.cholesky(gram_matrix)]
  transfers between devices with their start and end apart: 2 -> 0, of which waited for: 1 -> 0; matrix products, arithmetic and copies ran while one was open for 17% -> 0% of each run, Pallas kernels for 0% -> 0%
where the time goes in v1:
time: 107 us
  Pallas kernels  99.8 us (93%)
  local copies, waits for them, and re-layouts  6.41 us (6%)
    pallas_call x1, Pallas kernels, local(): pl.pallas_call(far_kernel, out_shape=(jax.ShapeDtypeStruct(block, f32), j...  90.2 us
    pallas_call x1, Pallas kernels, local(): pl.pallas_call(last_kernel, grid=(AMPS // tile,), out_shape=(jax.ShapeDty...  9.59 us
    unnamed x12, local copies, waits for them, and re-layouts  6.41 us

profile of v1, /device:TPU:1, one launch (start us, length us, event | category | flops | bytes accessed | tf_op | source)
XLA Modules:
  0.0 106.9 jit_solution(3725914664482453871)
XLA Ops:
  0.6 0.0 copy-start
  0.6 1.6 %copy-done = f32[32,16384]{1,0:T(8,128)S(1)} copy-done((f32[32,16384]{1,0:T(8,128)S(1)}, f32[32,16384]{1,0:T(8,128)}, u32[]{:S(2)}) %copy-start) | copy-done | bytes 2097176
  2.2 0.0 copy-start.1
  2.2 1.6 %copy-done.1 = f32[32,16384]{1,0:T(8,128)S(1)} copy-done((f32[32,16384]{1,0:T(8,128)S(1)}, f32[32,16384]{1,0:T(8,128)}, u32[]{:S(2)}) %copy-start.1) | copy-done | bytes 2097176
  3.8 0.0 copy-start.4
  3.8 0.7 copy-done.4
  4.5 0.0 copy-start.5
  4.5 0.7 copy-done.5
  5.1 90.2 %far_and_gram.1 = (f32[32,16384]{1,0:T(8,128)S(1)}, f32[8,128]{1,0:T(8,128)S(1)}) custom-call(s32[21]{0:T(128)S(1)} %copy-done.4, s32[20]{0:T(128)S(1)} %copy-done.5, f32[32,16384]{1,0:T(8,128)S(1)} %copy-done, f32[32,16384]{1,0:T(8,128)S(1)} %copy-done.1), custom_call_target="tpu_custom_call" | custom-call | tf_op jit(solution)/shard_map/far_and_gram/pallas_call | solution.py:350
  95.4 0.0 copy-start.2
  95.4 1.3 %copy-done.2 = f32[32,16384]{1,0:T(8,128)} copy-done((f32[32,16384]{1,0:T(8,128)}, f32[32,16384]{1,0:T(8,128)S(1)}, u32[]{:S(2)}) %copy-start.2) | copy-done | bytes 2097176
  96.7 0.0 copy-start.3
  96.7 0.6 copy-done.3
  97.3 9.6 %factor_and_apply.1 = (f32[32,16384]{1,0:T(8,128)}, f32[32,32]{1,0:T(8,128)}) custom-call(f32[8,128]{1,0:T(8,128)} %copy-done.3, f32[32,16384]{1,0:T(8,128)} %copy-done.2), custom_call_target="tpu_custom_call" | custom-call | tf_op jit(solution)/shard_map/factor_and_apply/pallas_call | solution.py:378
Async XLA Ops:
  0.6 1.6 %copy-start = (f32[32,16384]{1,0:T(8,128)S(1)}, f32[32,16384]{1,0:T(8,128)}, u32[]{:S(2)}) copy-start(f32[32,16384]{1,0:T(8,128)} %previous_hbm.1) | copy-start | bytes 6291460
  2.2 1.6 %copy-start.1 = (f32[32,16384]{1,0:T(8,128)S(1)}, f32[32,16384]{1,0:T(8,128)}, u32[]{:S(2)}) copy-start(f32[32,16384]{1,0:T(8,128)} %current_hbm.1) | copy-start | bytes 6291460
  3.8 0.7 copy-start.4
  4.5 0.7 copy-start.5
  95.4 1.4 %copy-start.2 = (f32[32,16384]{1,0:T(8,128)}, f32[32,16384]{1,0:T(8,128)S(1)}, u32[]{:S(2)}) copy-start(f32[32,16384]{1,0:T(8,128)S(1)} %get-tuple-element.5.filtered_ref) | copy-start | bytes 6291460
  96.7 0.6 copy-start.3

commit v2 on v1

--- a/solution.py
+++ b/solution.py
@@ -15,15 +15,17 @@
 SITES = 21
 SCALE = 4.0 / SITES
 CHUNKS = 16
+HOP = 2
 WIDTH = AMPS // CHUNKS
 TOPS = WIDTH // 128
-LEAD = 2
-LAST_LAG = 3
+LAST_LAG = 3 * HOP
+TILES = 4
+VMEM_LIMIT = 66000000
 
 
 def far_kernel(
-    field_ref, bond_ref, previous_hbm, current_hbm, filtered_hbm, gram_ref,
-    current, previous, filtered, weights, direct, ring_z, ring_x, gram, first, second,
+    field_hbm, bond_hbm, previous_hbm, current_hbm, filtered_hbm, gram_ref,
+    field_ref, bond_ref, current, previous, filtered, weights, direct, ring_z, ring_x, gram, first, second,
     load_sem, send_sem, relay_sem, direct_sem, z_sem, x_sem, small_send, first_sem, second_sem,
 ):
     hi = lax.axis_index("hi")
@@ -36,6 +38,10 @@
 
     load_current = pltpu.make_async_copy(current_hbm, current, load_sem.at[0])
     load_previous = pltpu.make_async_copy(previous_hbm, previous, load_sem.at[1])
+    load_field = pltpu.make_async_copy(field_hbm, field_ref, load_sem.at[2])
+    load_bond = pltpu.make_async_copy(bond_hbm, bond_ref, load_sem.at[3])
+    load_field.start()
+    load_bond.start()
     load_current.start()
     load_previous.start()
 
@@ -93,8 +99,8 @@
         return dict(
             active=role < 2, own=(own_device, jnp.where(role == 0, 0, 1)),
             relays=[
-                (has_a, a_device, jnp.where(role == 3, 0, 2), jnp.where(role == 3, 1, 2)),
-                (has_b, b_device, jnp.where(role == 3, 2, 1), jnp.where(role == 3, 2, 1)),
+                (has_a, a_device, jnp.where(role == 3, 0, 2), jnp.where(role == 3, HOP, 2 * HOP)),
+                (has_b, b_device, jnp.where(role == 3, 2, 1), jnp.where(role == 3, 2 * HOP, HOP)),
             ],
         )
 
@@ -131,18 +137,11 @@
             slot = plan["own"][1]
             when(plan["active"], lambda ring=ring, sems=sems, index=index, plan=plan, slot=slot:
                  own_copy(ring, cols, index, plan, sems.at[slot, k]).start())
-        when(takes[1], lambda: direct_copy(1, cols, direct_sem.at[1, k]).start())
-
-    @pl.loop(0, LEAD)
-    def _(k):
-        send_own(k)
-
-    @pl.loop(0, CHUNKS)
-    def _(k):
-        cols = columns(k)
-        for i in (2, 3, 4, 0):
+        for i in (1, 2, 3, 4, 0):
             when(takes[i], lambda i=i: direct_copy(i, cols, direct_sem.at[i, k]).start())
 
+    load_field.wait()
+    load_bond.wait()
     level = [bond_ref[s].astype(jnp.float32) for s in range(SITES - 1)]
     field = [0.75 * field_ref[s].astype(jnp.float32) for s in range(SITES)]
     half = [0.25 * v for v in level]
@@ -243,9 +242,9 @@
 
     @pl.loop(0, CHUNKS + LAST_LAG)
     def _(s):
-        @pl.when(s + LEAD < CHUNKS)
+        @pl.when(s < CHUNKS)
         def _():
-            send_own(s + LEAD)
+            send_own(s)
 
         for ring, sems, _, base, plan in plans:
             for which in range(2):
@@ -320,74 +319,104 @@
     store.wait()
 
 
-def last_kernel(gram_ref, filtered_ref, ortho_ref, upper_ref, inverse_ref):
-    @pl.when(pl.program_id(0) == 0)
-    def _():
-        packed = gram_ref[...]
-        parts = [packed] + [pltpu.roll(packed, 128 - 32 * i, 1) for i in range(1, 4)]
-        table = jnp.concatenate(parts, axis=0)
-        row = lax.broadcasted_iota(jnp.int32, (VECTORS, 128), 0)
-        lane = lax.broadcasted_iota(jnp.int32, (VECTORS, 128), 1)
-        table = jnp.where(lane < 32, table, jnp.where(lane - 32 == row, 1.0, 0.0))
-        for j in range(VECTORS - 1):
-            factor = table[:, j:j + 1] / table[j:j + 1, j:j + 1]
-            factor = jnp.where(row[:, 0:1] > j, factor, 0.0)
-            table = table - factor * table[j:j + 1, :]
-        pivots = jnp.sum(jnp.where(row == lane, table, 0.0), axis=1, keepdims=True)
-        table = table / jnp.sqrt(pivots)
-        upper_ref[...] = jnp.where(lane >= row, table, 0.0)[:, 0:32]
-        inverse_ref[...] = pltpu.roll(table, 96, 1)[:, 0:32]
-
-    ortho_ref[...] = jnp.dot(
-        inverse_ref[...], filtered_ref[...], precision=HIGHEST, preferred_element_type=jnp.float32
+def last_kernel(gram_ref, filtered_hbm, ortho_hbm, upper_ref, filtered, ortho, load_sem, store_sem):
+    tile = AMPS // TILES
+
+    def load(i):
+        cols = pl.ds(i * tile, tile)
+        return pltpu.make_async_copy(filtered_hbm.at[:, cols], filtered.at[:, cols], load_sem.at[i])
+
+    def store(i):
+        cols = pl.ds(i * tile, tile)
+        return pltpu.make_async_copy(ortho.at[:, cols], ortho_hbm.at[:, cols], store_sem.at[i])
+
+    for i in range(TILES):
+        load(i).start()
+
+    packed = gram_ref[...]
+    parts = [packed] + [pltpu.roll(packed, 128 - 32 * i, 1) for i in range(1, 4)]
+    table = jnp.concatenate(parts, axis=0)
+    row = lax.broadcasted_iota(jnp.int32, (VECTORS, 128), 0)
+    lane = lax.broadcasted_iota(jnp.int32, (VECTORS, 128), 1)
+    table = jnp.where(lane < 32, table, jnp.where(lane - 32 == row, 1.0, 0.0))
+    for j in range(VECTORS - 1):
+        factor = table[:, j:j + 1] / table[j:j + 1, j:j + 1]
+        factor = jnp.where(row[:, 0:1] > j, factor, 0.0)
+        table = table - factor * table[j:j + 1, :]
+    pivots = jnp.sum(jnp.where(row == lane, table, 0.0), axis=1, keepdims=True)
+    table = table / jnp.sqrt(pivots)
+    upper_ref[...] = jnp.where(lane >= row, table, 0.0)[:, 0:32]
+    inverse = pltpu.roll(table, 96, 1)[:, 0:32]
+
+    def split(values):
+        high = values.astype(jnp.bfloat16)
+        rest = values - high.astype(jnp.float32)
+        middle = rest.astype(jnp.bfloat16)
+        low = (rest - middle.astype(jnp.float32)).astype(jnp.bfloat16)
+        return high, middle, low
+
+    high, middle, low = split(inverse)
+    none = jnp.zeros_like(high)
+    left = jnp.concatenate(
+        [
+            jnp.concatenate([high, high, high], axis=1),
+            jnp.concatenate([middle, middle, none], axis=1),
+            jnp.concatenate([low, none, none], axis=1),
+        ],
+        axis=0,
     )
+    for i in range(TILES):
+        load(i).wait()
+        cols = pl.ds(i * tile, tile)
+        right = jnp.concatenate(split(filtered[:, cols]), axis=0)
+        parts = jnp.dot(left, right, preferred_element_type=jnp.float32)
+        ortho[:, cols] = parts[0:32] + (parts[32:64] + parts[64:96])
+        store(i).start()
+    for i in range(TILES):
+        store(i).wait()
 
 
 def local(previous, current, field_levels, bond_levels):
-    any_space = pl.BlockSpec(memory_space=pl.ANY)
+    hbm = pl.BlockSpec(memory_space=pltpu.HBM)
     block = (VECTORS, AMPS)
     f32 = jnp.float32
     filtered, gram = pl.pallas_call(
         far_kernel,
         out_shape=(jax.ShapeDtypeStruct(block, f32), jax.ShapeDtypeStruct((8, 128), f32)),
         in_specs=[
-            pl.BlockSpec(memory_space=pltpu.SMEM), pl.BlockSpec(memory_space=pltpu.SMEM),
-            any_space, any_space,
+            hbm, hbm, hbm, hbm,
         ],
-        out_specs=(any_space, pl.BlockSpec(memory_space=pltpu.VMEM)),
+        out_specs=(hbm, pl.BlockSpec(memory_space=pltpu.VMEM)),
         scratch_shapes=[
+            pltpu.SMEM((SITES,), jnp.int32), pltpu.SMEM((SITES - 1,), jnp.int32),
             pltpu.VMEM(block, f32), pltpu.VMEM(block, f32), pltpu.VMEM(block, f32),
             pltpu.VMEM((2, 256, 128), f32),
             pltpu.VMEM((5,) + block, f32), pltpu.VMEM((3,) + block, f32),
             pltpu.VMEM((3,) + block, f32),
             pltpu.VMEM((VECTORS, VECTORS), f32),
             pltpu.VMEM((8, 8, 128), f32), pltpu.VMEM((16, 8, 128), f32),
-            pltpu.SemaphoreType.DMA((2,)), pltpu.SemaphoreType.DMA((7,)),
+            pltpu.SemaphoreType.DMA((4,)), pltpu.SemaphoreType.DMA((7,)),
             pltpu.SemaphoreType.DMA((4,)), pltpu.SemaphoreType.DMA((5, CHUNKS)),
             pltpu.SemaphoreType.DMA((3, CHUNKS)), pltpu.SemaphoreType.DMA((3, CHUNKS)),
             pltpu.SemaphoreType.DMA((24,)), pltpu.SemaphoreType.DMA((8,)),
             pltpu.SemaphoreType.DMA((16,)),
         ],
         compiler_params=pltpu.CompilerParams(
-            collective_id=1, has_side_effects=True, vmem_limit_bytes=44 << 20
+            collective_id=1, has_side_effects=True, vmem_limit_bytes=VMEM_LIMIT
         ),
         name="far_and_gram",
     )(field_levels, bond_levels, previous, current)
-    tile = 2048
     return tuple(
         pl.pallas_call(
             last_kernel,
-            grid=(AMPS // tile,),
             out_shape=(jax.ShapeDtypeStruct(block, f32), jax.ShapeDtypeStruct((32, 32), f32)),
-            in_specs=[
-                pl.BlockSpec((8, 128), lambda i: (0, 0)),
-                pl.BlockSpec((VECTORS, tile), lambda i: (0, i)),
+            in_specs=[pl.BlockSpec(memory_space=pltpu.VMEM), hbm],
+            out_specs=(hbm, pl.BlockSpec(memory_space=pltpu.VMEM)),
+            scratch_shapes=[
+                pltpu.VMEM(block, f32), pltpu.VMEM(block, f32),
+                pltpu.SemaphoreType.DMA((TILES,)), pltpu.SemaphoreType.DMA((TILES,)),
             ],
-            out_specs=(
-                pl.BlockSpec((VECTORS, tile), lambda i: (0, i)),
-                pl.BlockSpec((32, 32), lambda i: (0, 0)),
-            ),
-            scratch_shapes=[pltpu.VMEM((32, 32), f32)],
+            compiler_params=pltpu.CompilerParams(vmem_limit_bytes=VMEM_LIMIT),
             name="factor_and_apply",
         )(gram, filtered)
     )

time: 107 us -> 82.3 us (0.77)
  Pallas kernels: 99.8 us -> 81.6 us
  local copies, waits for them, and re-layouts: 6.41 us -> 0 us
    pallas_call x1, Pallas kernels: 90.2 us -> 75.2 us  [local(): pl.pallas_call(far_kernel, out_shape=(jax.ShapeDtypeStruct(block, f32), j...]
    unnamed x12 -> x0, local copies, waits for them, and re-layouts: 6.41 us -> none
    pallas_call x1, Pallas kernels: 9.59 us -> 6.4 us  [local(): pl.pallas_call(last_kernel, out_shape=(jax.ShapeDtypeStruct(block, f32),...]
where the time goes in v2:
time: 82.3 us; the launch traced here: 82.2 us
  Pallas kernels  81.6 us (99%)
    pallas_call x1, Pallas kernels, local(): pl.pallas_call(far_kernel, out_shape=(jax.ShapeDtypeStruct(block, f32), j...  75.2 us
    pallas_call x1, Pallas kernels, local(): pl.pallas_call(last_kernel, out_shape=(jax.ShapeDtypeStruct(block, f32),...  6.4 us

profile of v2, /device:TPU:1, one launch (start us, length us, event | category | flops | bytes accessed | tf_op | source)
XLA Modules:
  0.0 82.2 jit_solution(10910687883262736187)
XLA Ops:
  0.6 75.2 %far_and_gram.1 = (f32[32,16384]{1,0:T(8,128)}, f32[8,128]{1,0:T(8,128)}) custom-call(s32[21]{0:T(128)} %field_hbm.1, s32[20]{0:T(128)} %bond_hbm.1, f32[32,16384]{1,0:T(8,128)} %previous_hbm.1, f32[32,16384]{1,0:T(8,128)} %current_hbm.1), custom_call_target="tpu_custom_call" | custom-call | tf_op jit(solution)/shard_map/far_and_gram/pallas_call | solution.py:383
  75.8 6.4 %factor_and_apply.1 = (f32[32,16384]{1,0:T(8,128)}, f32[32,32]{1,0:T(8,128)}) custom-call(f32[8,128]{1,0:T(8,128)} %get-tuple-element.4.gram_ref, f32[32,16384]{1,0:T(8,128)} %get-tuple-element.5.filtered_hbm), custom_call_target="tpu_custom_call" | custom-call | tf_op jit(solution)/shard_map/factor_and_apply/pallas_call | solution.py:410

commit v3 on v2

--- a/solution.py
+++ b/solution.py
@@ -50,7 +50,6 @@
         pl.semaphore_signal(barrier, inc=1, device_id=(hi, lo ^ i), device_id_type=MESH)
     for i in range(1, 16):
         pl.semaphore_signal(barrier, inc=1, device_id=(hi ^ i, lo), device_id_type=MESH)
-    pl.semaphore_wait(barrier, 22)
 
     def columns(k):
         return pl.ds(pl.multiple_of(k * WIDTH, WIDTH), WIDTH)
@@ -133,12 +132,17 @@
 
     def send_own(k):
         cols = columns(k)
+        for i in (1, 2, 3, 4, 0):
+            when(takes[i], lambda i=i: direct_copy(i, cols, direct_sem.at[i, k]).start())
+
+    def send_ring(s):
         for ring, sems, index, _, plan in plans:
             slot = plan["own"][1]
-            when(plan["active"], lambda ring=ring, sems=sems, index=index, plan=plan, slot=slot:
-                 own_copy(ring, cols, index, plan, sems.at[slot, k]).start())
-        for i in (1, 2, 3, 4, 0):
-            when(takes[i], lambda i=i: direct_copy(i, cols, direct_sem.at[i, k]).start())
+            k = s
+
+            @pl.when(plan["active"] & (k < CHUNKS))
+            def _(ring=ring, sems=sems, index=index, plan=plan, slot=slot, k=k):
+                own_copy(ring, columns(k), index, plan, sems.at[slot, k]).start()
 
     load_field.wait()
     load_bond.wait()
@@ -237,11 +241,12 @@
             preferred_element_type=jnp.float32,
         )
 
-    load_current.wait()
-    load_previous.wait()
+    pl.semaphore_wait(barrier, 22)
 
     @pl.loop(0, CHUNKS + LAST_LAG)
     def _(s):
+        send_ring(s)
+
         @pl.when(s < CHUNKS)
         def _():
             send_own(s)
@@ -261,6 +266,11 @@
 
         @pl.when(s < CHUNKS)
         def _():
+            @pl.when(s == 0)
+            def _():
+                load_current.wait()
+                load_previous.wait()
+
             local_part(s)
 
         @pl.when(s >= LAST_LAG)
@@ -319,7 +329,9 @@
     store.wait()
 
 
-def last_kernel(gram_ref, filtered_hbm, ortho_hbm, upper_ref, filtered, ortho, load_sem, store_sem):
+def last_kernel(
+    gram_ref, filtered_hbm, ortho_hbm, upper_hbm, filtered, ortho, upper, load_sem, store_sem, upper_sem
+):
     tile = AMPS // TILES
 
     def load(i):
@@ -345,7 +357,9 @@
         table = table - factor * table[j:j + 1, :]
     pivots = jnp.sum(jnp.where(row == lane, table, 0.0), axis=1, keepdims=True)
     table = table / jnp.sqrt(pivots)
-    upper_ref[...] = jnp.where(lane >= row, table, 0.0)[:, 0:32]
+    upper[...] = jnp.where(lane >= row, table, 0.0)[:, 0:32]
+    store_upper = pltpu.make_async_copy(upper, upper_hbm, upper_sem)
+    store_upper.start()
     inverse = pltpu.roll(table, 96, 1)[:, 0:32]
 
     def split(values):
@@ -374,6 +388,7 @@
         store(i).start()
     for i in range(TILES):
         store(i).wait()
+    store_upper.wait()
 
 
 def local(previous, current, field_levels, bond_levels):
@@ -411,10 +426,11 @@
             last_kernel,
             out_shape=(jax.ShapeDtypeStruct(block, f32), jax.ShapeDtypeStruct((32, 32), f32)),
             in_specs=[pl.BlockSpec(memory_space=pltpu.VMEM), hbm],
-            out_specs=(hbm, pl.BlockSpec(memory_space=pltpu.VMEM)),
+            out_specs=(hbm, hbm),
             scratch_shapes=[
-                pltpu.VMEM(block, f32), pltpu.VMEM(block, f32),
+                pltpu.VMEM(block, f32), pltpu.VMEM(block, f32), pltpu.VMEM((32, 32), f32),
                 pltpu.SemaphoreType.DMA((TILES,)), pltpu.SemaphoreType.DMA((TILES,)),
+                pltpu.SemaphoreType.DMA,
             ],
             compiler_params=pltpu.CompilerParams(vmem_limit_bytes=VMEM_LIMIT),
             name="factor_and_apply",

time: 82.3 us -> 81.3 us (0.988)
  Pallas kernels: 81.6 us -> 80.5 us
where the time goes in v3:
time: 81.3 us; the launch traced here: 81.1 us
  Pallas kernels  80.5 us (99%)
    pallas_call x1, Pallas kernels, local(): pl.pallas_call(far_kernel, out_shape=(jax.ShapeDtypeStruct(block, f32), j...  74.7 us
    pallas_call x1, Pallas kernels, local(): pl.pallas_call(last_kernel, out_shape=(jax.ShapeDtypeStruct(block, f32),...  5.81 us

profile of v3, /device:TPU:1, one launch (start us, length us, event | category | flops | bytes accessed | tf_op | source)
XLA Modules:
  0.0 81.1 jit_solution(13897243349815363308)
XLA Ops:
  0.6 74.7 %far_and_gram.1 = (f32[32,16384]{1,0:T(8,128)}, f32[8,128]{1,0:T(8,128)}) custom-call(s32[21]{0:T(128)} %field_hbm.1, s32[20]{0:T(128)} %bond_hbm.1, f32[32,16384]{1,0:T(8,128)} %previous_hbm.1, f32[32,16384]{1,0:T(8,128)} %current_hbm.1), custom_call_target="tpu_custom_call" | custom-call | tf_op jit(solution)/shard_map/far_and_gram/pallas_call | solution.py:398
  75.3 5.8 %factor_and_apply.1 = (f32[32,16384]{1,0:T(8,128)}, f32[32,32]{1,0:T(8,128)}) custom-call(f32[8,128]{1,0:T(8,128)} %get-tuple-element.4.gram_ref, f32[32,16384]{1,0:T(8,128)} %get-tuple-element.5.filtered_hbm), custom_call_target="tpu_custom_call" | custom-call | tf_op jit(solution)/shard_map/factor_and_apply/pallas_call | solution.py:425

commit v4 on v3

--- a/solution.py
+++ b/solution.py
@@ -19,7 +19,7 @@
 WIDTH = AMPS // CHUNKS
 TOPS = WIDTH // 128
 LAST_LAG = 3 * HOP
-TILES = 4
+TILES = (8192, 6144, 2048)
 VMEM_LIMIT = 66000000
 
 
@@ -65,7 +65,7 @@
 
     def direct_copy(i, cols, sem):
         return pltpu.make_async_remote_copy(
-            src_ref=current_hbm.at[:, cols], dst_ref=direct.at[i, :, cols],
+            src_ref=current.at[:, cols], dst_ref=direct.at[i, :, cols],
             send_sem=send_sem.at[i], recv_sem=sem, device_id=partners[i], device_id_type=MESH,
         )
 
@@ -111,7 +111,7 @@
     def own_copy(ring, k_cols, sem_index, plan, recv):
         device, slot = plan["own"]
         return pltpu.make_async_remote_copy(
-            src_ref=current_hbm.at[:, k_cols], dst_ref=ring.at[slot, :, k_cols],
+            src_ref=current.at[:, k_cols], dst_ref=ring.at[slot, :, k_cols],
             send_sem=send_sem.at[sem_index], recv_sem=recv, device_id=device, device_id_type=MESH,
         )
 
@@ -241,6 +241,7 @@
             preferred_element_type=jnp.float32,
         )
 
+    load_current.wait()
     pl.semaphore_wait(barrier, 22)
 
     @pl.loop(0, CHUNKS + LAST_LAG)
@@ -268,7 +269,6 @@
         def _():
             @pl.when(s == 0)
             def _():
-                load_current.wait()
                 load_previous.wait()
 
             local_part(s)
@@ -332,17 +332,17 @@
 def last_kernel(
     gram_ref, filtered_hbm, ortho_hbm, upper_hbm, filtered, ortho, upper, load_sem, store_sem, upper_sem
 ):
-    tile = AMPS // TILES
+    edges = [sum(TILES[:i]) for i in range(len(TILES))]
 
     def load(i):
-        cols = pl.ds(i * tile, tile)
+        cols = pl.ds(edges[i], TILES[i])
         return pltpu.make_async_copy(filtered_hbm.at[:, cols], filtered.at[:, cols], load_sem.at[i])
 
     def store(i):
-        cols = pl.ds(i * tile, tile)
+        cols = pl.ds(edges[i], TILES[i])
         return pltpu.make_async_copy(ortho.at[:, cols], ortho_hbm.at[:, cols], store_sem.at[i])
 
-    for i in range(TILES):
+    for i in range(len(TILES)):
         load(i).start()
 
     packed = gram_ref[...]
@@ -379,14 +379,14 @@
         ],
         axis=0,
     )
-    for i in range(TILES):
+    for i in range(len(TILES)):
         load(i).wait()
-        cols = pl.ds(i * tile, tile)
+        cols = pl.ds(edges[i], TILES[i])
         right = jnp.concatenate(split(filtered[:, cols]), axis=0)
         parts = jnp.dot(left, right, preferred_element_type=jnp.float32)
         ortho[:, cols] = parts[0:32] + (parts[32:64] + parts[64:96])
         store(i).start()
-    for i in range(TILES):
+    for i in range(len(TILES)):
         store(i).wait()
     store_upper.wait()
 
@@ -429,7 +429,7 @@
             out_specs=(hbm, hbm),
             scratch_shapes=[
                 pltpu.VMEM(block, f32), pltpu.VMEM(block, f32), pltpu.VMEM((32, 32), f32),
-                pltpu.SemaphoreType.DMA((TILES,)), pltpu.SemaphoreType.DMA((TILES,)),
+                pltpu.SemaphoreType.DMA((len(TILES),)), pltpu.SemaphoreType.DMA((len(TILES),)),
                 pltpu.SemaphoreType.DMA,
             ],
             compiler_params=pltpu.CompilerParams(vmem_limit_bytes=VMEM_LIMIT),

time: 81.3 us -> 80.8 us (level)
  no operation moved by 1% of the time
where the time goes in v4:
time: 80.8 us; the launch traced here: 80.7 us
  Pallas kernels  80.1 us (99%)
    pallas_call x1, Pallas kernels, local(): pl.pallas_call(far_kernel, out_shape=(jax.ShapeDtypeStruct(block, f32), j...  74.5 us
    pallas_call x1, Pallas kernels, local(): pl.pallas_call(last_kernel, out_shape=(jax.ShapeDtypeStruct(block, f32),...  5.55 us

profile of v4, /device:TPU:1, one launch (start us, length us, event | category | flops | bytes accessed | tf_op | source)
XLA Modules:
  0.0 80.7 jit_solution(2041176737383581862)
XLA Ops:
  0.6 74.5 %far_and_gram.1 = (f32[32,16384]{1,0:T(8,128)}, f32[8,128]{1,0:T(8,128)}) custom-call(s32[21]{0:T(128)} %field_hbm.1, s32[20]{0:T(128)} %bond_hbm.1, f32[32,16384]{1,0:T(8,128)} %previous_hbm.1, f32[32,16384]{1,0:T(8,128)} %current_hbm.1), custom_call_target="tpu_custom_call" | custom-call | tf_op jit(solution)/shard_map/far_and_gram/pallas_call | solution.py:398
  75.2 5.5 %factor_and_apply.1 = (f32[32,16384]{1,0:T(8,128)}, f32[32,32]{1,0:T(8,128)}) custom-call(f32[8,128]{1,0:T(8,128)} %get-tuple-element.4.gram_ref, f32[32,16384]{1,0:T(8,128)} %get-tuple-element.5.filtered_hbm), custom_call_target="tpu_custom_call" | custom-call | tf_op jit(solution)/shard_map/factor_and_apply/pallas_call | solution.py:425

commit v5 on v4

--- a/solution.py
+++ b/solution.py
@@ -366,25 +366,19 @@
         high = values.astype(jnp.bfloat16)
         rest = values - high.astype(jnp.float32)
         middle = rest.astype(jnp.bfloat16)
-        low = (rest - middle.astype(jnp.float32)).astype(jnp.bfloat16)
-        return high, middle, low
-
-    high, middle, low = split(inverse)
+        return high, middle
+
+    high, middle = split(inverse)
     none = jnp.zeros_like(high)
     left = jnp.concatenate(
-        [
-            jnp.concatenate([high, high, high], axis=1),
-            jnp.concatenate([middle, middle, none], axis=1),
-            jnp.concatenate([low, none, none], axis=1),
-        ],
-        axis=0,
+        [jnp.concatenate([high, high], axis=1), jnp.concatenate([middle, none], axis=1)], axis=0
     )
     for i in range(len(TILES)):
         load(i).wait()
         cols = pl.ds(edges[i], TILES[i])
         right = jnp.concatenate(split(filtered[:, cols]), axis=0)
         parts = jnp.dot(left, right, preferred_element_type=jnp.float32)
-        ortho[:, cols] = parts[0:32] + (parts[32:64] + parts[64:96])
+        ortho[:, cols] = parts[0:32] + parts[32:64]
         store(i).start()
     for i in range(len(TILES)):
         store(i).wait()

time: 80.8 us -> 80.6 us (level)
  no operation moved by 1% of the time
where the time goes in v5:
time: 80.6 us; the launch traced here: 80.4 us
  Pallas kernels  79.8 us (99%)
    pallas_call x1, Pallas kernels, local(): pl.pallas_call(far_kernel, out_shape=(jax.ShapeDtypeStruct(block, f32), j...  74.5 us
    pallas_call x1, Pallas kernels, local(): pl.pallas_call(last_kernel, out_shape=(jax.ShapeDtypeStruct(block, f32),...  5.25 us

profile of v5, /device:TPU:1, one launch (start us, length us, event | category | flops | bytes accessed | tf_op | source)
XLA Modules:
  0.0 80.4 jit_solution(14496893257940570239)
XLA Ops:
  0.6 74.5 %far_and_gram.1 = (f32[32,16384]{1,0:T(8,128)}, f32[8,128]{1,0:T(8,128)}) custom-call(s32[21]{0:T(128)} %field_hbm.1, s32[20]{0:T(128)} %bond_hbm.1, f32[32,16384]{1,0:T(8,128)} %previous_hbm.1, f32[32,16384]{1,0:T(8,128)} %current_hbm.1), custom_call_target="tpu_custom_call" | custom-call | tf_op jit(solution)/shard_map/far_and_gram/pallas_call | solution.py:392
  75.2 5.2 %factor_and_apply.1 = (f32[32,16384]{1,0:T(8,128)}, f32[32,32]{1,0:T(8,128)}) custom-call(f32[8,128]{1,0:T(8,128)} %get-tuple-element.4.gram_ref, f32[32,16384]{1,0:T(8,128)} %get-tuple-element.5.filtered_hbm), custom_call_target="tpu_custom_call" | custom-call | tf_op jit(solution)/shard_map/factor_and_apply/pallas_call | solution.py:419
